TPU v7x, 256 devices: a whole 4x4x8 slice. The times are simulated.
256 devices in a mesh: seq: 64 (over y, z, core), tp: 4 (over x).
Axes of the slice: x: 4, y: 4, z: 8, core: 2. Of those that a mesh axis runs over, the one named last changes fastest.
Arguments:
- short_hidden: bfloat16 [1024, 1280], P('seq', 'tp'), may hold values from -6 to 6
- long_hidden: bfloat16 [4, 1280], P(None, 'tp'), may hold values from -6 to 6
- short_len: int32 [1024], replicated, may hold values from 1 to 127
- short_slot: int32 [1024], replicated, may hold values from 0 to 2047, as said below
- w_query: bfloat16 [1280, 1280], P(None, 'tp'), may hold values from -0.15625 to 0.15625
- w_key: bfloat16 [1280, 1280], P(None, 'tp'), may hold values from -0.15625 to 0.15625
- w_value: bfloat16 [1280, 1280], P(None, 'tp'), may hold values from -0.15625 to 0.15625
- w_out: bfloat16 [1280, 1280], P('tp'), may hold values from -0.15625 to 0.15625
- qk_gain: float32 [1280], P('tp'), may hold values from 0.7 to 2
- step_rate: float32 [1280], replicated, may hold values from 0.1 to 0.6
- short_keys: bfloat16 [2048, 128, 1280], P('seq', None, 'tp'), may hold values from -0.19921875 to 0.19921875
- short_values: bfloat16 [2048, 128, 1280], P('seq', None, 'tp'), may hold values from -6 to 6
- long_keys: bfloat16 [4, 32768, 1280], P(None, 'seq', 'tp'), may hold values from -0.19921875 to 0.19921875
- long_values: bfloat16 [4, 32768, 1280], P(None, 'seq', 'tp'), may hold values from -6 to 6
Outputs:
- short_out: bfloat16 [1024, 1280], P('seq', 'tp')
- long_out: bfloat16 [4, 1280], P(None, 'tp')
Inputs may be any that keep to these rules, and one draw needn't show every extreme that they name: `short_slot`: all slot numbers are distinct; slot s is row s of short_keys and short_values, so it lies on index s // 32 of seq. In every draw some index of seq has all 32 of its slots taken.
All inputs are finite; a program needn't handle non-finite values.
Results may differ from a plain program's by a relative error of at most 0.01.
Values may be sent and summed in bfloat16 or wider, within the bound.
A program may use at most 64 MiB of HBM per device.

v0:
```python
import math
import jax
import jax.numpy as jnp
from jax import lax
from jax.sharding import PartitionSpec as P

HEAD = 64
EPS = 1e-06


def head_unit(x, gain):
    count = x.shape[0]
    parts = x.reshape(count, -1, HEAD)
    parts = parts * lax.rsqrt(jnp.sum(parts * parts, -1, keepdims=True) + EPS)
    return parts.reshape(count, -1) * gain


def row_unit(x):
    return x * lax.rsqrt(jnp.mean(x * x, -1, keepdims=True) + EPS)


def cache_terms(query, keys, values, live):
    batch, positions, width = keys.shape
    key_heads = keys.reshape(batch, positions, width // HEAD, HEAD)
    value_heads = values.reshape(batch, positions, width // HEAD, HEAD)
    query_heads = query.reshape(batch, width // HEAD, HEAD)
    scores = jnp.einsum(
        "bhe,bphe->bhp", query_heads, key_heads, preferred_element_type=jnp.float32
    ) * math.sqrt(HEAD)
    weights = jnp.where(live[:, None, :], jnp.exp(scores), jnp.float32(0.0))
    den = jnp.sum(weights, -1)
    num = jnp.einsum(
        "bhp,bphe->bhe",
        weights.astype(jnp.bfloat16),
        value_heads,
        preferred_element_type=jnp.float32,
    )
    return (num.reshape(batch, width), den)


def on_device(
    short_hidden,
    long_hidden,
    short_len,
    short_slot,
    w_query,
    w_key,
    w_value,
    w_out,
    qk_gain,
    step_rate,
    short_keys,
    short_values,
    long_keys,
    long_values,
):
    full_short, full_long = (
        lax.all_gather(short_hidden, "tp", axis=1, tiled=True),
        lax.all_gather(long_hidden, "tp", axis=1, tiled=True),
    )
    rows = jnp.concatenate([full_short, full_long], 0)
    n_short = full_short.shape[0]
    count = rows.shape[0]
    width = w_query.shape[1]
    head_count = width // HEAD
    q_proj = jnp.dot(rows, w_query, preferred_element_type=jnp.float32)
    k_proj = jnp.dot(rows, w_key, preferred_element_type=jnp.float32)
    v_proj = jnp.dot(rows, w_value, preferred_element_type=jnp.float32)
    query = head_unit(q_proj, qk_gain).astype(jnp.bfloat16)
    new_key = head_unit(k_proj, qk_gain).astype(jnp.bfloat16)
    new_value = v_proj.astype(jnp.bfloat16)
    all_queries = lax.all_gather(query[:n_short], "seq", axis=0, tiled=True)
    total_short = all_queries.shape[0]
    seq_index = lax.axis_index("seq")
    slot_dev = short_keys.shape[0]
    capacity = short_keys.shape[1]
    local_ids = seq_index * slot_dev + jnp.arange(slot_dev, dtype=jnp.int32)
    match = short_slot[None, :] == local_ids[:, None]
    owner = jnp.sum(jnp.where(match, jnp.arange(total_short, dtype=jnp.int32)[None, :], 0), 1)
    filled = jnp.any(match, 1)
    slot_query = jnp.where(
        filled[:, None], jnp.take(all_queries, owner, axis=0), jnp.zeros((), jnp.bfloat16)
    )
    slot_len = jnp.where(filled, jnp.take(short_len, owner, axis=0), 0)
    live = jnp.arange(capacity, dtype=jnp.int32)[None, :] < slot_len[:, None]
    slot_num, slot_den = cache_terms(slot_query, short_keys, short_values, live)
    home_slot = lax.dynamic_slice_in_dim(short_slot, seq_index * n_short, n_short)
    every_num, every_den = (
        lax.all_gather(slot_num.astype(jnp.bfloat16), "seq", axis=0, tiled=True).astype(
            slot_num.dtype
        ),
        lax.all_gather(slot_den.astype(jnp.bfloat16), "seq", axis=0, tiled=True).astype(
            slot_den.dtype
        ),
    )
    short_num = jnp.take(every_num, home_slot, axis=0)
    short_den = jnp.take(every_den, home_slot, axis=0)
    long_count = full_long.shape[0]
    long_live = jnp.ones((long_count, long_keys.shape[1]), dtype=bool)
    long_part_num, long_part_den = cache_terms(query[n_short:], long_keys, long_values, long_live)
    long_num, long_den = lax.psum((long_part_num, long_part_den), "seq")
    cache_num = jnp.concatenate([short_num, long_num], 0).reshape(count, head_count, HEAD)
    cache_den = jnp.concatenate([short_den, long_den], 0)
    query_heads = query.reshape(count, head_count, HEAD)
    key_heads = new_key.reshape(count, head_count, HEAD)
    value_heads = new_value.reshape(count, head_count, HEAD).astype(jnp.float32)
    own = jnp.exp(
        jnp.einsum("rhe,rhe->rh", query_heads, key_heads, preferred_element_type=jnp.float32)
        * math.sqrt(HEAD)
    )
    den = cache_den + own
    num = cache_num + own.astype(jnp.bfloat16).astype(jnp.float32)[..., None] * value_heads
    attended = (num / den[..., None]).reshape(count, width).astype(jnp.bfloat16)
    partial_proj = jnp.dot(attended, w_out, preferred_element_type=jnp.float32)
    tp_index = lax.axis_index("tp")
    proj = lax.psum(partial_proj.astype(jnp.bfloat16), "tp").astype(jnp.float32)
    state = rows.astype(jnp.float32)
    update = state + step_rate * (row_unit(proj) - state)
    result = lax.dynamic_slice_in_dim(row_unit(update), tp_index * width, width, 1)
    result = result.astype(jnp.bfloat16)
    return (result[:n_short], result[n_short:])


def solution(mesh):
    return jax.shard_map(
        on_device,
        mesh=mesh,
        in_specs=(
            P("seq", "tp"),
            P(None, "tp"),
            P(),
            P(),
            P(None, "tp"),
            P(None, "tp"),
            P(None, "tp"),
            P("tp", None),
            P("tp"),
            P(),
            P("seq", None, "tp"),
            P("seq", None, "tp"),
            P(None, "seq", "tp"),
            P(None, "seq", "tp"),
        ),
        out_specs=(P("seq", "tp"), P(None, "tp")),
        check_vma=False,
    )
```

profile of v0, /device:TPU:8, one launch (start us, length us, event | category | flops | bytes accessed | tf_op | source)
XLA Modules:
  0.0 436.6 jit_solution(15223891977575141921)
XLA Ops:
  7.3 1.0 fusion.5
  8.3 0.9 compare_reduce_fusion
  9.2 1.4 gather_fusion
  10.7 12.4 %all-gather.1 = bf16[4,320,4]{1,2,0:T(4,128)(2,1)S(1)} all-gather(bf16[1,320,4]{1,2,0:T(4,128)(2,1)} %bitcast.82), channel_id=1, replica_groups=mesh['seq'=64,'tp'=4] {'tp'}, dimensions={0}, use_global_device_ids=true | all-gather | bytes 12800 | tf_op jit(solution)/shard_map/all_gather | solution.py:59
  23.2 12.1 %all-gather = bf16[4,320,16]{1,2,0:T(8,128)(2,1)S(1)} all-gather(bf16[1,320,16]{1,2,0:T(8,128)(2,1)} %bitcast.80), channel_id=1, replica_groups=mesh['seq'=64,'tp'=4] {'tp'}, dimensions={0}, use_global_device_ids=true | all-gather | bytes 51200 | tf_op jit(solution)/shard_map/all_gather | solution.py:58
  35.4 1.5 fusion.39
  37.3 1.5 fusion.38
  39.1 53.5 %all_gather.17 = bf16[1024,320]{1,0:T(8,128)(2,1)S(1)} all-gather(bf16[16,320]{1,0:T(8,128)(2,1)S(1)} %slice.24), channel_id=1, replica_groups=mesh['seq'=64,'tp'=4] {'seq'}, dimensions={0}, use_global_device_ids=true | all-gather | bytes 665600 | tf_op jit(solution)/shard_map/all_gather | solution.py:72
  92.7 0.6 gather_fusion.1
  93.4 0.1 select_bitcast_fusion
  93.6 0.8 fusion.13
  94.3 0.1 fusion.17
  94.5 0.7 copy-done.3
  95.1 1.5 fusion.11
  96.6 0.7 convert_element_type.59
  97.4 1.6 fusion.40
  99.0 0.1 fusion.27
  99.1 1.8 fusion.19
  101.0 214.0 %all-reduce = (f32[4,5]{0,1:T(8,128)S(1)}, f32[4,320]{1,0:T(4,128)S(1)}) all-reduce(f32[4,5]{0,1:T(8,128)S(1)} %get-tuple-element.13, f32[4,320]{1,0:T(4,128)S(1)} %reshape.148), channel_id=1, replica_groups=mesh['seq'=64,'tp'=4] {'seq'}, use_global_device_ids=true, to_apply=%region_7.8 | all-reduce | flops 1300 | bytes 10400 | tf_op jit(solution)/shard_map/psum | solution.py:101
  315.4 82.4 %all-gather.2 = bf16[64,32,5]{1,2,0:T(8,128)(2,1)S(1)} all-gather(bf16[1,32,5]{1,2,0:T(8,128)(2,1)S(1)} %bitcast.81), channel_id=1, replica_groups=mesh['seq'=64,'tp'=4] {'seq'}, dimensions={0}, use_global_device_ids=true | all-gather | bytes 20800 | tf_op jit(solution)/shard_map/all_gather | solution.py:92
  397.8 0.1 copy.41
  397.9 1.8 copy.60
  399.8 0.8 compare_and_fusion.1
  400.5 1.8 gather_fusion.3
  403.1 3.3 convert_element_type.60
  406.4 2.5 gather_fusion.2
  408.9 2.1 convolution_convert_fusion
  411.1 17.1 %psum.23 = bf16[20,1280]{1,0:T(8,128)(2,1)S(1)} all-reduce(bf16[20,1280]{1,0:T(8,128)(2,1)S(1)} %convolution_convert_fusion), channel_id=1, replica_groups=mesh['seq'=64,'tp'=4] {'tp'}, use_global_device_ids=true, to_apply=%region_8.9 | all-reduce | flops 25600 | bytes 102400 | tf_op jit(solution)/shard_map/psum | solution.py:116
  428.2 0.1 fusion.7
  428.3 0.2 multiply_reduce_fusion
  428.6 0.6 slice.27
  429.2 0.6 slice.26
  (55 shorter events, 2.7 us)
Async XLA Ops:
  7.2 86.4 %copy-start = (bf16[32,128,320]{1,2,0:T(8,128)(2,1)S(1)}, bf16[32,128,320]{1,2,0:T(8,128)(2,1)}, u32[]{:S(2)}) copy-start(bf16[32,128,320]{1,2,0:T(8,128)(2,1)} %param.24) | copy-start | bytes 7864324
  7.2 31.9 %copy-start.2 = (f32[320]{0:T(512)S(1)}, f32[320]{0:T(512)}, u32[]{:S(2)}) copy-start(f32[320]{0:T(512)} %param.22) | copy-start | bytes 3844
  7.2 395.9 %all-gather.5.cloned.1.call-start = ((), (), s32[]{:S(2)}) async-start(), calls=%async_computation | async-start | bytes 1597440 | tf_op jit(solution)/shard_map/all_gather | solution.py:89
  93.4 1.7 copy-start.3
  403.1 25.2 %copy-start.1 = (f32[1280]{0:T(1024)S(1)}, f32[1280]{0:T(1024)}, u32[]{:S(2)}) copy-start(f32[1280]{0:T(1024)} %param.23) | copy-start | bytes 15364
Sparse Core Ops, SparseCore 0:
  97.5 73.4 all-gather.4
where the time goes:
time: 437 us
  blocking collectives  392 us (90%)
  between operations  14.3 us (3%)
  local copies, waits for them, and re-layouts  12.6 us (3%)
  matrix products  10.7 us (2%)
  other arithmetic  7.42 us (2%)
    psum x1, blocking collectives, on_device(): long_num, long_den = lax.psum((long_part_num, long_part_den), 'seq')  214 us
    all_gather x1, blocking collectives, on_device(): lax.all_gather(slot_den.astype(jnp.bfloat16), 'seq', axis=0, tiled=True)  82.4 us
    all_gather x1, blocking collectives, on_device(): all_queries = lax.all_gather(query[:n_short], 'seq', axis=0, tiled=True)  53.5 us
    psum x1, blocking collectives, on_device(): proj = lax.psum(partial_proj.astype(jnp.bfloat16), 'tp').astype(jnp.float32)  17.1 us
    all_gather x1, blocking collectives, on_device(): lax.all_gather(long_hidden, 'tp', axis=1, tiled=True)  12.4 us
    all_gather x1, blocking collectives, on_device(): lax.all_gather(short_hidden, 'tp', axis=1, tiled=True)  12.1 us
  transfers between devices with their start and end apart: 1, of which 0 were waited for; matrix products, arithmetic and copies ran while one was open for 2% of the time, Pallas kernels for 0%

commit v1 on v0

--- a/solution.py
+++ b/solution.py
@@ -89,9 +89,12 @@
         lax.all_gather(slot_num.astype(jnp.bfloat16), "seq", axis=0, tiled=True).astype(
             slot_num.dtype
         ),
-        lax.all_gather(slot_den.astype(jnp.bfloat16), "seq", axis=0, tiled=True).astype(
-            slot_den.dtype
-        ),
+        jnp.concatenate(
+            lax.all_to_all(
+                jnp.stack([slot_den.astype(jnp.bfloat16)] * lax.axis_size("seq")), "seq", 0, 0
+            ),
+            axis=0,
+        ).astype(slot_den.dtype),
     )
     short_num = jnp.take(every_num, home_slot, axis=0)
     short_den = jnp.take(every_den, home_slot, axis=0)

time: 437 us -> 398 us (0.911)
  the two profiles are of different devices: /device:TPU:8 before, /device:TPU:4 now
where the time goes in v1:
time: 398 us
  blocking collectives  345 us (87%)
  between operations  14.3 us (4%)
  local copies, waits for them, and re-layouts  13.3 us (3%)
  matrix products  10.7 us (3%)
  other arithmetic  7.43 us (2%)
  starting transfers between devices  6.78 us (2%)
    psum x1, blocking collectives, on_device(): long_num, long_den = lax.psum((long_part_num, long_part_den), 'seq')  251 us
    all_gather x1, blocking collectives, on_device(): all_queries = lax.all_gather(query[:n_short], 'seq', axis=0, tiled=True)  52.6 us
    psum x1, blocking collectives, on_device(): proj = lax.psum(partial_proj.astype(jnp.bfloat16), 'tp').astype(jnp.float32)  17.1 us
    all_gather x1, blocking collectives, on_device(): lax.all_gather(short_hidden, 'tp', axis=1, tiled=True)  12.2 us
    all_gather x1, blocking collectives, on_device(): lax.all_gather(long_hidden, 'tp', axis=1, tiled=True)  12.1 us
  transfers between devices with their start and end apart: 2, of which 0 were waited for; matrix products, arithmetic and copies ran while one was open for 2% of the time, Pallas kernels for 0%

profile of v1, /device:TPU:4, one launch (start us, length us, event | category | flops | bytes accessed | tf_op | source)
XLA Modules:
  0.0 397.6 jit_solution(171430743132727998)
XLA Ops:
  7.3 1.0 fusion.5
  8.3 0.9 compare_reduce_fusion
  9.2 1.4 gather_fusion
  10.7 12.1 %all-gather.1 = bf16[4,320,4]{1,2,0:T(4,128)(2,1)S(1)} all-gather(bf16[1,320,4]{1,2,0:T(4,128)(2,1)} %bitcast.78), channel_id=1, replica_groups=mesh['seq'=64,'tp'=4] {'tp'}, dimensions={0}, use_global_device_ids=true | all-gather | bytes 12800 | tf_op jit(solution)/shard_map/all_gather | solution.py:59
  22.9 12.2 %all-gather = bf16[4,320,16]{1,2,0:T(8,128)(2,1)S(1)} all-gather(bf16[1,320,16]{1,2,0:T(8,128)(2,1)} %bitcast.77), channel_id=1, replica_groups=mesh['seq'=64,'tp'=4] {'tp'}, dimensions={0}, use_global_device_ids=true | all-gather | bytes 51200 | tf_op jit(solution)/shard_map/all_gather | solution.py:58
  35.2 1.5 fusion.39
  37.1 1.5 fusion.38
  38.9 52.6 %all_gather.14 = bf16[1024,320]{1,0:T(8,128)(2,1)S(1)} all-gather(bf16[16,320]{1,0:T(8,128)(2,1)S(1)} %slice.24), channel_id=1, replica_groups=mesh['seq'=64,'tp'=4] {'seq'}, dimensions={0}, use_global_device_ids=true | all-gather | bytes 665600 | tf_op jit(solution)/shard_map/all_gather | solution.py:72
  91.6 0.6 gather_fusion.1
  92.3 0.1 select_bitcast_fusion
  92.5 0.8 fusion.13
  93.3 0.1 fusion.17
  93.4 0.7 copy-done.3
  94.1 1.5 fusion.11
  95.5 0.7 convert_element_type.64
  96.3 0.7 stack.2
  96.9 6.7 %all-to-all-start = ((bf16[64,32,5]{1,2,0:T(8,128)(2,1)}), bf16[64,32,5]{1,2,0:T(8,128)(2,1)S(1)}, u32[]{:S(2)}, u32[]{:S(2)}) async-start(bf16[64,32,5]{1,2,0:T(8,128)(2,1)} %stack.2), calls=%async_computation | async-start | bytes 262144 | tf_op jit(solution)/shard_map/all_to_all | solution.py:93
  104.0 0.8 compare_and_fusion.1
  104.8 1.6 fusion.40
  106.5 1.8 fusion.19
  108.4 251.1 %all-reduce = (f32[4,5]{0,1:T(8,128)S(1)}, f32[4,320]{1,0:T(4,128)S(1)}) all-reduce(f32[4,5]{0,1:T(8,128)S(1)} %get-tuple-element.13, f32[4,320]{1,0:T(4,128)S(1)} %reshape.153), channel_id=1, replica_groups=mesh['seq'=64,'tp'=4] {'seq'}, use_global_device_ids=true, to_apply=%region_7.8 | all-reduce | flops 1300 | bytes 10400 | tf_op jit(solution)/shard_map/psum | solution.py:104
  359.6 0.1 copy.41
  359.7 1.8 copy.60
  361.5 1.8 gather_fusion.3
  364.1 3.3 convert_element_type.65
  367.4 2.5 gather_fusion.2
  369.9 2.1 convolution_convert_fusion
  372.1 17.1 %psum.23 = bf16[20,1280]{1,0:T(8,128)(2,1)S(1)} all-reduce(bf16[20,1280]{1,0:T(8,128)(2,1)S(1)} %convolution_convert_fusion), channel_id=1, replica_groups=mesh['seq'=64,'tp'=4] {'tp'}, use_global_device_ids=true, to_apply=%region_8.9 | all-reduce | flops 25600 | bytes 102400 | tf_op jit(solution)/shard_map/psum | solution.py:119
  389.1 0.1 fusion.7
  389.3 0.2 multiply_reduce_fusion
  389.6 0.6 slice.27
  390.2 0.6 slice.26
  (57 shorter events, 2.8 us)
Async XLA Ops:
  7.2 85.3 %copy-start = (bf16[32,128,320]{1,2,0:T(8,128)(2,1)S(1)}, bf16[32,128,320]{1,2,0:T(8,128)(2,1)}, u32[]{:S(2)}) copy-start(bf16[32,128,320]{1,2,0:T(8,128)(2,1)} %param.24) | copy-start | bytes 7864324
  7.2 31.7 %copy-start.2 = (f32[320]{0:T(512)S(1)}, f32[320]{0:T(512)}, u32[]{:S(2)}) copy-start(f32[320]{0:T(512)} %param.22) | copy-start | bytes 3844
  7.2 356.9 %all-gather.4.cloned.1.call-start = ((), (), s32[]{:S(2)}) async-start(), calls=%async_computation.1 | async-start | bytes 1597440 | tf_op jit(solution)/shard_map/all_gather | solution.py:89
  92.3 1.7 copy-start.3
  96.9 262.7 %all-to-all-start = ((bf16[64,32,5]{1,2,0:T(8,128)(2,1)}), bf16[64,32,5]{1,2,0:T(8,128)(2,1)S(1)}, u32[]{:S(2)}, u32[]{:S(2)}) async-start(bf16[64,32,5]{1,2,0:T(8,128)(2,1)} %stack.2), calls=%async_computation | async-start | bytes 262144 | tf_op jit(solution)/shard_map/all_to_all | solution.py:93
  364.1 25.2 %copy-start.1 = (f32[1280]{0:T(1024)S(1)}, f32[1280]{0:T(1024)}, u32[]{:S(2)}) copy-start(f32[1280]{0:T(1024)} %param.23) | copy-start | bytes 15364
Sparse Core Ops, SparseCore 0:
  96.4 75.4 all-gather.3
